TPU v7x, 32 devices: a whole 2x2x4 slice. The times are simulated.
32 devices in a mesh: groups: 2 (over x), tm: 16 (over z, y, core).
Axes of the slice: x: 2, y: 2, z: 4, core: 2. Of those that a mesh axis runs over, the one named last changes fastest.
Arguments:
- states: bfloat16 [4096, 2, 1024], P('tm', 'groups'), parts along dimension 1, may hold values from -6 to 6
- goals: bfloat16 [4096, 2, 1024], P('tm', 'groups'), parts along dimension 1, may hold values from -6 to 6
- pos_offset: int32 [16, 2, 8], P('tm', 'groups'), parts along dimension 1, may hold values from 0 to 15
- neg_blocks: int32 [16, 2, 16], P('tm', 'groups'), parts along dimension 1, may hold values from 0 to 15
Outputs:
- loss_mean: float32 [2], P('groups'), parts along dimension 0
- grad_states: float32 [4096, 2, 1024], P('tm', 'groups'), parts along dimension 1
- grad_goals: float32 [4096, 2, 1024], P('tm', 'groups'), parts along dimension 1
There are 2 independent parts, one for each index of `groups`. A program takes and returns all parts, laid end to end along the dimension named above; each array names one. Nothing has to cross between parts.
All inputs are finite; a program needn't handle non-finite values.
Results may differ from a plain program's by a relative error of at most 0.012.
Values may be sent and summed in bfloat16 or wider, within the bound.
No kernel may reach another device: no remote copies, remote signals or barrier semaphores. Data moves between devices by JAX's collectives and lax.ppermute only.
A program may use at most 128 MiB of HBM per device.

v0:
```python
import math
import jax
import jax.numpy as jnp
from jax import lax
from jax.sharding import PartitionSpec as P

E = 1024
L = 256


def pair_weights(pos_offset, neg_blocks, row_first, row_count, col_count):
    block_count = row_count // L
    row_blocks = row_first // L + jnp.arange(block_count, dtype=jnp.int32)
    col_times = jnp.arange(col_count, dtype=jnp.int32)
    col_blocks = col_times // L
    targets = row_blocks[:, None, None] + pos_offset
    pos_count = jnp.sum((targets[..., None] == col_blocks).astype(jnp.float32), axis=2)
    neg_count = jnp.sum((neg_blocks[..., None] == col_blocks).astype(jnp.float32), axis=2)
    pos_count = jnp.repeat(jnp.swapaxes(pos_count, 0, 1), L, axis=1)
    neg_count = jnp.repeat(jnp.swapaxes(neg_count, 0, 1), L, axis=1)
    row_times = row_first + jnp.arange(row_count, dtype=jnp.int32)
    later_mask = (col_times[None, :] > row_times[:, None]).astype(jnp.float32)
    return (pos_count * later_mask, neg_count)


def score_terms(anchor_rows, goal_rows, pos_weight, neg_weight):
    inv_root = 1.0 / math.sqrt(E)
    scores = (
        jnp.einsum("qte,kte->tqk", anchor_rows, goal_rows, preferred_element_type=jnp.float32)
        * inv_root
    )
    loss_sum = jnp.sum(pos_weight * jax.nn.softplus(-scores) + neg_weight * jax.nn.softplus(scores))
    slopes = neg_weight * jax.nn.sigmoid(scores) - pos_weight * jax.nn.sigmoid(-scores)
    return (loss_sum, (slopes * inv_root).astype(jnp.bfloat16))


def per_device(states, goals, pos_offset, neg_blocks):
    row_count = states.shape[0]
    traj_count = states.shape[1]
    steps_all = row_count * lax.axis_size("tm")
    row_first = lax.axis_index("tm") * row_count
    goal_piece = lax.all_gather(goals, "tm", axis=0, tiled=True)
    col_count = goal_piece.shape[0]
    pos_weight, neg_weight = pair_weights(pos_offset, neg_blocks, row_first, row_count, col_count)
    loss_sum, coeffs = score_terms(states, goal_piece, pos_weight, neg_weight)
    grad_rows = jnp.einsum("tqk,kte->qte", coeffs, goal_piece, preferred_element_type=jnp.float32)
    loss_sum, coeffs, grad_rows = (loss_sum, coeffs, grad_rows)
    folded = (grad_rows, loss_sum, coeffs)
    grad_states = folded[0]
    loss_sum = folded[1]
    coeff_all = folded[2]
    grad_goals = lax.psum_scatter(
        jnp.einsum("tqk,qte->kte", coeff_all, states, preferred_element_type=jnp.float32).astype(
            jnp.bfloat16
        ),
        "tm",
        scatter_dimension=0,
        tiled=True,
    ).astype(jnp.float32)
    loss_all = lax.psum(loss_sum, "tm")
    loss_mean = (loss_all / (traj_count * steps_all)).reshape(1)
    return (loss_mean, grad_states, grad_goals)


def solution(mesh):
    in_specs = (
        P("tm", "groups", None),
        P("tm", "groups", None),
        P("tm", "groups", None),
        P("tm", "groups", None),
    )
    out_specs = (P("groups"), P("tm", "groups", None), P("tm", "groups", None))
    return jax.shard_map(
        per_device, mesh=mesh, in_specs=in_specs, out_specs=out_specs, check_vma=False
    )
```

profile of v0, /device:TPU:0, one launch (start us, length us, event | category | flops | bytes accessed | tf_op | source)
XLA Modules:
  0.0 219.8 jit_solution(17836653208547374864)
XLA Ops:
  7.2 0.0 copy-start
  7.2 0.0 all-gather.2.cloned.1.call-start
  7.2 0.7 all-gather.2.cloned.1.call-update
  7.9 0.0 reduce-scatter.2.cloned.1.call-start
  8.0 0.7 add_bitcast_fusion
  8.7 0.1 convert_reduce_fusion.1
  8.8 0.8 convert_reduce_fusion
  9.6 77.6 %all-gather.2.cloned.1.call-done = bf16[4096,1,1024]{2,0,1:T(8,128)(2,1)} async-done(((bf16[256,1,1024]{2,0,1:T(8,128)(2,1)}), bf16[4096,1,1024]{2,0,1:T(8,128)(2,1)}) %all-gather.2.cloned.1.call-update) | async-done | bytes 8388624 | tf_op jit(solution)/shard_map/all_gather | solution.py:42
  87.2 0.0 copy-done
  87.2 11.5 %fusion.8 = (f32[]{:T(128)}, f32[256,4096]{1,0:T(8,128)S(1)}) fusion(f32[4096]{0:T(1024)S(1)} %convert_reduce_fusion, f32[4096]{0:T(1024)S(1)} %convert_reduce_fusion.1, s32[256]{0:T(256)S(1)} %iota_add_fusion, bf16[4096,1,1024]{2,0,1:T(8,128)(2,1)} %all-gather.2.cloned.1.call-done, bf16[256,1,1024]{2,0,1:T(8,128)(2,1)S(1)} %copy-done), kind=kOutput, calls=%fused_computation.11 | convolution fusion | flops 2168455168 | bytes 13140996 | tf_op jit(solution)/shard_map/qte,kte->tqk/dot_general | solution.py:29
  98.7 0.0 copy-start.1
  98.7 1.9 copy-done.1
  100.6 6.2 %convert_bitcast_fusion = bf16[4096,1,1024]{2,0,1:T(8,128)(2,1)} fusion(bf16[256,1,1024]{2,0,1:T(8,128)(2,1)S(1)} %copy-done, f32[256,4096]{1,0:T(8,128)S(1)} %get-tuple-element.10, f32[4096]{0:T(1024)S(1)} %convert_reduce_fusion, f32[4096]{0:T(1024)S(1)} %convert_reduce_fusion.1, s32[256]{0:T(256)S(1)} %iota_add_fusion), kind=kOutput, calls=%fused_computation.6 | convolution fusion | flops 2164260864 | bytes 13140992 | tf_op jit(solution)/shard_map/tqk,qte->kte/dot_general | solution.py:53
  106.8 0.0 reduce-scatter.2.cloned.1.call-update
  106.8 32.1 %psum.7 = f32[]{:T(128)} all-reduce(f32[]{:T(128)} %get-tuple-element.9), channel_id=1, replica_groups=mesh['groups'=2,'tm'=16] {'tm'}, use_global_device_ids=true, to_apply=%region_3.4 | all-reduce | flops 1 | bytes 8 | tf_op jit(solution)/shard_map/psum | solution.py:60
  138.9 8.2 %fusion.13 = f32[256,1,1024]{2,0,1:T(8,128)S(1)} fusion(bf16[4096,1,1024]{2,0,1:T(8,128)(2,1)} %all-gather.2.cloned.1.call-done, f32[256,4096]{1,0:T(8,128)} %copy-done.1, f32[4096]{0:T(1024)S(1)} %convert_reduce_fusion, f32[4096]{0:T(1024)S(1)} %convert_reduce_fusion.1, s32[256]{0:T(256)S(1)} %iota_add_fusion), kind=kOutput, calls=%fused_computation.18 | convolution fusion | flops 2160066560 | bytes 13665280 | tf_op jit(solution)/shard_map/tqk,kte->qte/dot_general | solution.py:46
  147.1 2.0 copy.9
  149.8 59.2 %reduce-scatter.2.cloned.1.call-done = bf16[256,1,1024]{2,0,1:T(8,128)(2,1)} async-done(((bf16[4096,1,1024]{2,0,1:T(8,128)(2,1)}), bf16[256,1,1024]{2,0,1:T(8,128)(2,1)}) %reduce-scatter.2.cloned.1.call-update) | async-done | bytes 524304 | tf_op jit(solution)/shard_map/reduce_scatter | solution.py:52
  209.0 2.8 %copy.10 = f32[256,1,1024]{2,1,0:T(1,128)} copy(bf16[256,1,1024]{2,0,1:T(8,128)(2,1)} %reduce-scatter.2.cloned.1.call-done) | data formatting | bytes 1572864
  (2 shorter events, 0.0 us)
Async XLA Ops:
  7.2 80.0 %copy-start = (bf16[256,1,1024]{2,0,1:T(8,128)(2,1)S(1)}, bf16[256,1,1024]{2,0,1:T(8,128)(2,1)}, u32[]{:S(2)}) copy-start(bf16[256,1,1024]{2,0,1:T(8,128)(2,1)} %param.4) | copy-start | bytes 1572868
  7.2 80.0 %all-gather.2.cloned.1.call-start = ((), (), s32[]{:S(2)}) async-start(), calls=%async_computation.1 | async-start | bytes 8912896 | tf_op jit(solution)/shard_map/all_gather | solution.py:42
  7.9 201.1 %reduce-scatter.2.cloned.1.call-start = ((), (), s32[]{:S(2)}) async-start(), calls=%async_computation.2 | async-start | bytes 8912896 | tf_op jit(solution)/shard_map/reduce_scatter | solution.py:52
  98.7 1.9 copy-start.1
Sparse Core Ops, SparseCore 0:
  10.2 77.0 all-gather.1
  107.0 102.0 reduce-scatter.1
where the time goes:
time: 220 us
  waiting for transfers between devices  138 us (63%)
  blocking collectives  32.1 us (15%)
  matrix products  25.9 us (12%)
  between operations  15.9 us (7%)
  local copies, waits for them, and re-layouts  6.8 us (3%)
    all_gather x1, waiting for transfers between devices, per_device(): goal_piece = lax.all_gather(goals, 'tm', axis=0, tiled=True)  77.6 us
    reduce_scatter x1, waiting for transfers between devices, per_device(): lax.psum_scatter(jnp.einsum('tqk,qte->kte', coeff_all, states, preferred_...  59.2 us
    psum x1, blocking collectives, per_device(): loss_all = lax.psum(loss_sum, 'tm')  32.1 us
    dot_general x1, matrix products, score_terms(): jnp.einsum('qte,kte->tqk', anchor_rows, goal_rows, preferred_element_type...  11.5 us
    dot_general x1, matrix products, per_device(): jnp.einsum('tqk,kte->qte', coeffs, goal_piece, preferred_element_type=jnp...  8.22 us
    unnamed x6, local copies, waits for them, and re-layouts  6.8 us
    dot_general x1, matrix products, per_device(): jnp.einsum('tqk,qte->kte', coeff_all, states, preferred_element_type=jnp....  6.2 us
  transfers between devices with their start and end apart: 2, of which 2 were waited for; matrix products, arithmetic and copies ran while one was open for 5% of the time, Pallas kernels for 0%

commit v1 on v0

--- a/solution.py
+++ b/solution.py
@@ -6,6 +6,12 @@
 
 E = 1024
 L = 256
+
+
+def tiled_gather(x, axis, dim):
+    peers = lax.axis_size(axis)
+    repeats = [peers if d == dim else 1 for d in range(x.ndim)]
+    return lax.all_to_all(jnp.tile(x, repeats), axis, split_axis=dim, concat_axis=dim, tiled=True)
 
 
 def pair_weights(pos_offset, neg_blocks, row_first, row_count, col_count):
@@ -39,7 +45,7 @@
     traj_count = states.shape[1]
     steps_all = row_count * lax.axis_size("tm")
     row_first = lax.axis_index("tm") * row_count
-    goal_piece = lax.all_gather(goals, "tm", axis=0, tiled=True)
+    goal_piece = tiled_gather(goals, "tm", 0)
     col_count = goal_piece.shape[0]
     pos_weight, neg_weight = pair_weights(pos_offset, neg_blocks, row_first, row_count, col_count)
     loss_sum, coeffs = score_terms(states, goal_piece, pos_weight, neg_weight)

time: 220 us -> 387 us (1.76)
  waiting for transfers between devices: 138 us -> 206 us
  local copies, waits for them, and re-layouts: 6.8 us -> 43.7 us
  blocking collectives: 32.1 us -> 65.5 us
  other arithmetic: 1.56 us -> 12.9 us
  matrix products: 25.9 us -> 34 us
  starting transfers between devices: 0.08 us -> 7.82 us
    all_to_all x0 -> x1, waiting for transfers between devices: none -> 150 us  [tiled_gather(): lax.all_to_all(jnp.tile(x, repeats), axis, split_axis=dim, concat_axis=di...]
    all_gather x1 -> x0, waiting for transfers between devices: 77.6 us -> none  [per_device(): goal_piece = lax.all_gather(goals, 'tm', axis=0, tiled=True)]
    psum x1, blocking collectives: 32.1 us -> 65.5 us  [per_device(): loss_all = lax.psum(loss_sum, 'tm')]
    unnamed x6 -> x14, local copies, waits for them, and re-layouts: 6.8 us -> 37.8 us
    another operation x0 -> x1, other arithmetic: none -> 12.7 us  [tiled_gather(): jnp.tile(x, repeats)]
    all_to_all x0 -> x1, starting transfers between devices: none -> 7.6 us  [tiled_gather(): lax.all_to_all(jnp.tile(x, repeats), axis, split_axis=dim, concat_axis=di...]
    another operation x0 -> x2, local copies, waits for them, and re-layouts: none -> 5.9 us  [tiled_gather(): jnp.tile(x, repeats)]
    dot_general x1, matrix products: 11.5 us -> 16.4 us  [score_terms(): jnp.einsum('qte,kte->tqk', anchor_rows, goal_rows, preferred_element_type...]
  transfers between devices with their start and end apart: 2 -> 2, of which waited for: 2 -> 2; matrix products, arithmetic and copies ran while one was open for 5% -> 4% of each run, Pallas kernels for 0% -> 0%
where the time goes in v1:
time: 387 us; the launch traced here: 386 us
  waiting for transfers between devices  206 us (53%)
  blocking collectives  65.5 us (17%)
  local copies, waits for them, and re-layouts  43.7 us (11%)
  matrix products  34 us (9%)
  between operations  15.9 us (4%)
  other arithmetic  12.9 us (3%)
  starting transfers between devices  7.82 us (2%)
    all_to_all x1, waiting for transfers between devices, tiled_gather(): lax.all_to_all(jnp.tile(x, repeats), axis, split_axis=dim, concat_axis=di...  150 us
    psum x1, blocking collectives, per_device(): loss_all = lax.psum(loss_sum, 'tm')  65.5 us
    reduce_scatter x1, waiting for transfers between devices, per_device(): lax.psum_scatter(jnp.einsum('tqk,qte->kte', coeff_all, states, preferred_...  55.9 us
    unnamed x14, local copies, waits for them, and re-layouts  37.8 us
    dot_general x1, matrix products, score_terms(): jnp.einsum('qte,kte->tqk', anchor_rows, goal_rows, preferred_element_type...  16.4 us
    another operation x1, other arithmetic, tiled_gather(): jnp.tile(x, repeats)  12.7 us
    dot_general x1, matrix products, per_device(): jnp.einsum('tqk,kte->qte', coeffs, goal_piece, preferred_element_type=jnp...  11.4 us
  transfers between devices with their start and end apart: 2, of which 2 were waited for; matrix products, arithmetic and copies ran while one was open for 4% of the time, Pallas kernels for 0%

profile of v1, /device:TPU:0, one launch (start us, length us, event | category | flops | bytes accessed | tf_op | source)
XLA Modules:
  0.0 385.7 jit_solution(15526041602857871771)
XLA Ops:
  7.2 0.0 copy-start
  7.2 5.4 %tile.12 = bf16[16,256,1024]{2,1,0:T(8,128)(2,1)} broadcast(bf16[256,1024]{1,0:T(8,128)(2,1)} %bitcast.37), dimensions={1,2} | broadcast | bytes 8912896 | tf_op jit(solution)/shard_map/tile | solution.py:14
  12.6 0.5 broadcast.169
  13.1 12.7 %reduce.4 = bf16[4096,1024]{1,0:T(8,128)(2,1)} reduce(bf16[4096,1,1024]{2,0,1:T(8,128)(2,1)} %bitcast.36, bf16[]{:T(256)} %broadcast.169), dimensions={1}, to_apply=%copy.14.reduce_sub_computation | reduce | bytes 16777218 | tf_op jit(solution)/shard_map/tile | solution.py:14
  25.8 14.5 %reshape.226 = bf16[16,2,131072]{2,1,0:T(2,128)(2,1)} reshape(bf16[4096,1024]{1,0:T(8,128)(2,1)} %reduce.4) | data formatting | bytes 16777216
  40.3 0.0 copy-start.3
  40.3 0.0 copy-start.2
  40.3 7.6 %all-to-all-start = ((bf16[16,2,131072]{2,1,0:T(2,128)(2,1)}), bf16[16,2,131072]{2,1,0:T(2,128)(2,1)}, u32[]{:S(2)}, u32[]{:S(2)}) async-start(bf16[16,2,131072]{2,1,0:T(2,128)(2,1)} %reshape.226), calls=%async_computation | async-start | bytes 16777216 | tf_op jit(solution)/shard_map/all_to_all | solution.py:14
  47.9 0.2 reduce-scatter.2.cloned.1.call-start
  48.2 0.0 copy-done.3
  48.2 0.1 convert_reduce_fusion.1
  48.3 0.0 copy-done.2
  48.3 0.1 convert_reduce_fusion
  48.4 150.0 %all-to-all-done = bf16[16,2,131072]{2,1,0:T(2,128)(2,1)} async-done(((bf16[16,2,131072]{2,1,0:T(2,128)(2,1)}), bf16[16,2,131072]{2,1,0:T(2,128)(2,1)}, u32[]{:S(2)}, u32[]{:S(2)}) %all-to-all-start) | async-done | bytes 8388640 | tf_op jit(solution)/shard_map/all_to_all | solution.py:14
  198.5 16.4 %reshape.227 = bf16[4096,1,1024]{2,1,0:T(2,128)(2,1)} reshape(bf16[16,2,131072]{2,1,0:T(2,128)(2,1)} %all-to-all-done) | data formatting | bytes 16777216
  214.8 0.0 copy-done
  214.8 16.4 %fusion.8 = (f32[]{:T(128)}, f32[256,4096]{1,0:T(8,128)S(1)}) fusion(f32[4096]{0:T(1024)S(1)} %convert_reduce_fusion, f32[4096]{0:T(1024)S(1)} %convert_reduce_fusion.1, s32[256]{0:T(256)S(1)} %iota_add_fusion, bf16[4096,1,1024]{2,1,0:T(2,128)(2,1)} %reshape.227, bf16[256,1,1024]{2,0,1:T(8,128)(2,1)S(1)} %copy-done), kind=kOutput, calls=%fused_computation.11 | convolution fusion | flops 2168455168 | bytes 13140996 | tf_op jit(solution)/shard_map/qte,kte->tqk/dot_general | solution.py:35
  231.2 0.0 copy-start.4
  231.2 2.0 copy-done.4
  233.2 6.2 %convert_bitcast_fusion = bf16[4096,1,1024]{2,0,1:T(8,128)(2,1)} fusion(bf16[256,1,1024]{2,0,1:T(8,128)(2,1)S(1)} %copy-done, f32[256,4096]{1,0:T(8,128)S(1)} %get-tuple-element.16, f32[4096]{0:T(1024)S(1)} %convert_reduce_fusion, f32[4096]{0:T(1024)S(1)} %convert_reduce_fusion.1, s32[256]{0:T(256)S(1)} %iota_add_fusion), kind=kOutput, calls=%fused_computation.6 | convolution fusion | flops 2164260864 | bytes 13140992 | tf_op jit(solution)/shard_map/tqk,qte->kte/dot_general | solution.py:59
  239.4 0.0 reduce-scatter.2.cloned.1.call-update
  239.4 65.5 %psum.7 = f32[]{:T(128)} all-reduce(f32[]{:T(128)} %get-tuple-element.15), channel_id=1, replica_groups=mesh['groups'=2,'tm'=16] {'tm'}, use_global_device_ids=true, to_apply=%region_3.4 | all-reduce | flops 1 | bytes 8 | tf_op jit(solution)/shard_map/psum | solution.py:66
  304.9 0.0 copy-start.1
  304.9 11.4 %fusion.15 = f32[256,1,1024]{2,0,1:T(8,128)S(1)} fusion(bf16[4096,1,1024]{2,1,0:T(2,128)(2,1)} %reshape.227, f32[256,4096]{1,0:T(8,128)} %copy-done.4, f32[4096]{0:T(1024)S(1)} %convert_reduce_fusion, f32[4096]{0:T(1024)S(1)} %convert_reduce_fusion.1, s32[256]{0:T(256)S(1)} %iota_add_fusion), kind=kOutput, calls=%fused_computation.20 | convolution fusion | flops 2160066560 | bytes 13665280 | tf_op jit(solution)/shard_map/tqk,kte->qte/dot_general | solution.py:52
  316.3 2.0 copy.15
  319.0 55.9 %reduce-scatter.2.cloned.1.call-done = bf16[256,1,1024]{2,0,1:T(8,128)(2,1)} async-done(((bf16[4096,1,1024]{2,0,1:T(8,128)(2,1)}), bf16[256,1,1024]{2,0,1:T(8,128)(2,1)}) %reduce-scatter.2.cloned.1.call-update) | async-done | bytes 524304 | tf_op jit(solution)/shard_map/reduce_scatter | solution.py:58
  374.9 2.8 copy.16
  377.7 0.0 copy-done.1
  (3 shorter events, 0.0 us)
Async XLA Ops:
  7.2 207.7 %copy-start = (bf16[256,1,1024]{2,0,1:T(8,128)(2,1)S(1)}, bf16[256,1,1024]{2,0,1:T(8,128)(2,1)}, u32[]{:S(2)}) copy-start(bf16[256,1,1024]{2,0,1:T(8,128)(2,1)} %param.4) | copy-start | bytes 1572868
  40.3 7.9 %copy-start.3 = (s32[1,1,8]{2,1,0:T(1,128)S(1)}, s32[1,1,8]{2,1,0:T(1,128)}, u32[]{:S(2)}) copy-start(s32[1,1,8]{2,1,0:T(1,128)} %param.6) | copy-start | bytes 100
  40.3 8.0 %copy-start.2 = (s32[1,1,16]{2,1,0:T(1,128)S(1)}, s32[1,1,16]{2,1,0:T(1,128)}, u32[]{:S(2)}) copy-start(s32[1,1,16]{2,1,0:T(1,128)} %param.7) | copy-start | bytes 196
  40.3 158.2 %all-to-all-start = ((bf16[16,2,131072]{2,1,0:T(2,128)(2,1)}), bf16[16,2,131072]{2,1,0:T(2,128)(2,1)}, u32[]{:S(2)}, u32[]{:S(2)}) async-start(bf16[16,2,131072]{2,1,0:T(2,128)(2,1)} %reshape.226), calls=%async_computation | async-start | bytes 16777216 | tf_op jit(solution)/shard_map/all_to_all | solution.py:14
  47.9 327.0 %reduce-scatter.2.cloned.1.call-start = ((), (), s32[]{:S(2)}) async-start(), calls=%async_computation.2 | async-start | bytes 8912896 | tf_op jit(solution)/shard_map/reduce_scatter | solution.py:58
  231.2 2.0 copy-start.4
  304.9 72.8 %copy-start.1 = (bf16[256,1,1024]{2,0,1:T(8,128)(2,1)S(1)}, bf16[256,1,1024]{2,0,1:T(8,128)(2,1)}, u32[]{:S(2)}) copy-start(bf16[256,1,1024]{2,0,1:T(8,128)(2,1)} %param.4) | copy-start | bytes 1572868
Sparse Core Ops, SparseCore 0:
  239.5 135.2 reduce-scatter.1
